TPU v7x, 32 devices: a whole 2x2x4 slice. The times are simulated.
32 devices in a mesh: pages: 2 (over y), tile: 4 (over z), mp: 2 (over x), batch: 2 (over core).
Axes of the slice: x: 2, y: 2, z: 4, core: 2. Of those that a mesh axis runs over, the one named last changes fastest.
Arguments:
- page_cells: bfloat16 [4, 48, 24, 1024], P(('pages', 'batch'), 'tile'), parts along dimension 0, may hold values from -40 to 40
- text_states: bfloat16 [4, 1024, 1024], P(('pages', 'batch'), 'tile'), parts along dimension 0, may hold values from -40 to 40
- enc_query: bfloat16 [1024, 1024], P('batch', 'mp'), may hold values from -2.5 to 2.5
- enc_keyval: bfloat16 [1024, 2, 1024], P('batch', None, 'mp'), may hold values from -0.1875 to 0.1875
- enc_proj: bfloat16 [1024, 1024], P('mp', 'batch'), may hold values from -0.1875 to 0.1875
- dec_query: bfloat16 [1024, 1024], P('batch', 'mp'), may hold values from -2.5 to 2.5
- dec_keyval: bfloat16 [1024, 2, 1024], P('batch', None, 'mp'), may hold values from -0.1875 to 0.1875
- dec_out: bfloat16 [1024, 1024], P('mp', 'batch'), may hold values from -0.1875 to 0.1875
Outputs:
- encoded: bfloat16 [4, 48, 24, 1024], P(('pages', 'batch'), 'tile'), parts along dimension 0
- decoded: bfloat16 [4, 1024, 1024], P(('pages', 'batch'), ('tile', 'mp')), parts along dimension 0
There are 2 independent parts, one for each index of `pages`. A program takes and returns all parts, laid end to end along the dimension named above; an argument that names none is the same for every part. Nothing has to cross between parts.
All inputs are finite; a program needn't handle non-finite values.
Results may differ from a plain program's by a relative error of at most 0.012.
Values may be sent and summed in bfloat16 or wider, within the bound.
No kernel may reach another device: no remote copies, remote signals or barrier semaphores. Data moves between devices by JAX's collectives and lax.ppermute only.
A program may use at most 64 MiB of HBM per device.

v0:
```python
import math
import jax
import jax.numpy as jnp
from jax import lax
from jax.sharding import PartitionSpec as P

HEAD_ENC = 32
HEAD_DEC = 64


def from_behind(value, axis, by):
    devices = lax.axis_size(axis)
    return lax.ppermute(value, axis, [(i, (i + by) % devices) for i in range(devices)])


def layer_norm(values):
    center = values - jnp.mean(values, axis=-1, keepdims=True)
    variance = jnp.mean(center * center, axis=-1, keepdims=True)
    return center / jnp.sqrt(variance + 1e-05)


def regions(length, window, offset):
    index_row = jnp.arange(length, dtype=jnp.int32)
    return jnp.where(
        index_row < length - window, 0, jnp.where(index_row < length - offset, 1, 2)
    ).astype(jnp.int32)


def body(page_cells, text_states, enc_query, enc_keyval, enc_proj, dec_query, dec_keyval, dec_out):
    wq_enc, wkv_enc, wproj_enc, wq_dec, wkv_dec, wout_dec = (
        lax.all_gather(enc_query, "batch", axis=0, tiled=True),
        lax.all_gather(enc_keyval, "batch", axis=0, tiled=True),
        lax.all_gather(enc_proj, "batch", axis=1, tiled=True),
        lax.all_gather(dec_query, "batch", axis=0, tiled=True),
        lax.all_gather(dec_keyval, "batch", axis=0, tiled=True),
        lax.all_gather(dec_out, "batch", axis=1, tiled=True),
    )
    pages_here, window, columns, width = page_cells.shape
    offset = window // 2
    own_rows = window * columns
    hq_enc = wq_enc.shape[1]
    heads_enc = hq_enc // HEAD_ENC
    joined = jnp.concatenate([wq_enc, wkv_enc.reshape(width, 2 * hq_enc)], axis=1)
    rows_below = from_behind(page_cells[:, :offset], "tile", -1)
    normed = layer_norm(
        jnp.concatenate([page_cells[:, offset:], rows_below], axis=1).astype(jnp.float32)
    ).astype(jnp.bfloat16)
    projected = jnp.einsum(
        "prcd,de->prce", normed, joined, preferred_element_type=jnp.float32
    ).astype(jnp.bfloat16)
    projected = jnp.roll(projected, -offset, axis=2)
    per_row = columns // window
    shaped = projected.reshape(pages_here, window, per_row, window, 3, heads_enc, HEAD_ENC)
    shaped = jnp.swapaxes(shaped, 1, 2).reshape(
        pages_here, per_row, window * window, 3, heads_enc, HEAD_ENC
    )
    win_q = shaped[:, :, :, 0]
    win_k = shaped[:, :, :, 1]
    win_v = shaped[:, :, :, 2]
    is_last = lax.axis_index("tile") == lax.axis_size("tile") - 1
    local_rows = jnp.arange(window, dtype=jnp.int32)
    row_region = jnp.where(is_last, jnp.where(local_rows < window - offset, 1, 2), 0).astype(
        jnp.int32
    )
    labels = row_region[:, None] * 3 + regions(columns, window, offset)[None, :]
    labels = jnp.swapaxes(labels.reshape(window, per_row, window), 0, 1).reshape(
        per_row, window * window
    )
    allowed = labels[:, :, None] == labels[:, None, :]
    win_scores = jnp.einsum(
        "pnqhd,pnkhd->pnhqk", win_q, win_k, preferred_element_type=jnp.float32
    ) / math.sqrt(HEAD_ENC)
    win_scores = jnp.where(allowed[None, :, None], win_scores, -jnp.inf)
    top = jnp.max(win_scores, axis=-1, keepdims=True)
    expd = jnp.exp(win_scores - top)
    win_weights = (expd / jnp.sum(expd, axis=-1, keepdims=True)).astype(jnp.bfloat16)
    win_out = jnp.einsum(
        "pnhqk,pnkhd->pnqhd", win_weights, win_v, preferred_element_type=jnp.float32
    ).astype(jnp.bfloat16)
    win_out = win_out.reshape(pages_here, per_row, window, window, hq_enc)
    win_out = jnp.swapaxes(win_out, 1, 2).reshape(pages_here, window, columns, hq_enc)
    win_out = jnp.roll(win_out, offset, axis=2)
    rows_above = from_behind(win_out[:, window - offset :], "tile", 1)
    unrolled = jnp.concatenate([rows_above, win_out[:, : window - offset]], axis=1)
    partial_proj = jnp.einsum(
        "prce,ed->prcd", unrolled, wproj_enc, preferred_element_type=jnp.float32
    )
    summed = lax.psum(partial_proj.astype(jnp.bfloat16), "mp").astype(jnp.float32)
    encoded = (page_cells.astype(jnp.float32) + summed).astype(jnp.bfloat16)
    hq_dec = wq_dec.shape[1]
    heads_dec = hq_dec // HEAD_DEC
    page_normed = (
        layer_norm(encoded.astype(jnp.float32))
        .astype(jnp.bfloat16)
        .reshape(pages_here, own_rows, width)
    )
    page_kv = jnp.einsum(
        "pnd,de->pne",
        page_normed,
        wkv_dec.reshape(width, 2 * hq_dec),
        preferred_element_type=jnp.float32,
    ).astype(jnp.bfloat16)
    text_normed = layer_norm(text_states.astype(jnp.float32)).astype(jnp.bfloat16)
    queries = jnp.einsum(
        "ptd,de->pte", text_normed, wq_dec, preferred_element_type=jnp.float32
    ).astype(jnp.bfloat16)
    text_len = text_states.shape[1]
    query_heads = queries.reshape(pages_here, text_len, heads_dec, HEAD_DEC)
    start_state = (
        jnp.full((pages_here, heads_dec, text_len), -jnp.inf, jnp.float32),
        jnp.zeros((pages_here, heads_dec, text_len), jnp.float32),
        jnp.zeros((pages_here, heads_dec, text_len, HEAD_DEC), jnp.float32),
    )
    carried = start_state
    shard_rows = lax.all_gather(page_kv, "tile", axis=1, tiled=True)
    count = shard_rows.shape[1] // own_rows
    grouped = max(
        (
            factor
            for factor in range(1, count + 1)
            if count % factor == 0 and factor * own_rows <= 2048
        )
    )
    blocks = jnp.moveaxis(
        shard_rows.reshape(pages_here, count // grouped, grouped * own_rows, 2 * hq_dec), 1, 0
    )

    def advance(running, block_kv):
        maxima, totals, accum = running
        span = block_kv.shape[1]
        block_keys = block_kv[..., :hq_dec].reshape(pages_here, span, heads_dec, HEAD_DEC)
        block_vals = block_kv[..., hq_dec:].reshape(pages_here, span, heads_dec, HEAD_DEC)
        cross_scores = jnp.einsum(
            "pqhd,pkhd->phqk", query_heads, block_keys, preferred_element_type=jnp.float32
        ) / math.sqrt(HEAD_DEC)
        newest = jnp.maximum(maxima, jnp.max(cross_scores, axis=-1))
        rescale = jnp.exp(maxima - newest)
        expo = jnp.exp(cross_scores - newest[..., None])
        totals = totals * rescale + jnp.sum(expo, axis=-1)
        accum = accum * rescale[..., None] + jnp.einsum(
            "phqk,pkhd->phqd",
            expo.astype(jnp.bfloat16),
            block_vals,
            preferred_element_type=jnp.float32,
        )
        return ((newest, totals, accum), None)

    carried, unused = lax.scan(advance, carried, blocks)
    maxima, totals, accum = carried
    context = (
        jnp.transpose(accum / totals[..., None], (0, 2, 1, 3))
        .reshape(pages_here, text_len, hq_dec)
        .astype(jnp.bfloat16)
    )
    share = text_len // lax.axis_size("mp")
    mixed = lax.psum_scatter(
        jnp.einsum("pte,ed->tpd", context, wout_dec, preferred_element_type=jnp.float32).astype(
            jnp.bfloat16
        ),
        "mp",
        scatter_dimension=0,
        tiled=True,
    ).astype(jnp.float32)
    own_text = lax.dynamic_slice_in_dim(text_states, lax.axis_index("mp") * share, share, 1)
    decoded = (own_text.astype(jnp.float32) + jnp.moveaxis(mixed, 0, 1)).astype(jnp.bfloat16)
    return (encoded, decoded)


def solution(mesh):
    placed = (
        P(("pages", "batch"), "tile", None, None),
        P(("pages", "batch"), "tile", None),
        P("batch", "mp"),
        P("batch", None, "mp"),
        P("mp", "batch"),
        P("batch", "mp"),
        P("batch", None, "mp"),
        P("mp", "batch"),
    )
    return jax.shard_map(
        body,
        mesh=mesh,
        in_specs=placed,
        out_specs=(
            P(("pages", "batch"), "tile", None, None),
            P(("pages", "batch"), ("tile", "mp"), None),
        ),
        check_vma=False,
    )
```

profile of v0, /device:TPU:0, one launch (start us, length us, event | category | flops | bytes accessed | tf_op | source)
XLA Modules:
  0.0 199.5 jit_solution(16749749369688853707)
XLA Ops:
  7.2 0.7 all-gather.11.cloned.1.call-update
  7.9 0.0 all-gather.9.cloned.1.call-start
  8.0 0.7 all-gather.9.cloned.1.call-update
  8.7 0.7 all-gather.13.cloned.1.call-update
  9.4 0.1 fusion.80
  9.6 5.1 %collective-permute-start = (bf16[1,6,24,1024]{3,2,1,0:T(8,128)(2,1)S(1)}, bf16[1,6,24,1024]{3,2,1,0:T(8,128)(2,1)S(1)}, u32[]{:S(2)}, u32[]{:S(2)}) collective-permute-start(bf16[1,6,24,1024]{3,2,1,0:T(8,128)(2,1)S(1)} %get-tuple-element.29), channel_id=1, source_target_pairs={{0,12},{4,0},{8,4},{12,8},{1,13},{5,1},{9,5},{13,9},{2,14},{6,2},{... | collective-permute-start | bytes 884744 | tf_op jit(solution)/shard_map/ppermute | solution.py:13
  14.7 0.0 all-reduce.2.cloned.1.call-start
  14.8 0.1 add.86
  14.9 0.1 add.82
  14.9 0.1 add.83
  15.0 0.7 broadcast_compare_fusion
  15.8 5.1 %collective-permute-done = bf16[1,6,24,1024]{3,2,1,0:T(8,128)(2,1)S(1)} collective-permute-done((bf16[1,6,24,1024]{3,2,1,0:T(8,128)(2,1)S(1)}, bf16[1,6,24,1024]{3,2,1,0:T(8,128)(2,1)S(1)}, u32[]{:S(2)}, u32[]{:S(2)}) %collective-permute-start) | collective-permute-done | bytes 294944 | tf_op jit(solution)/shard_map/ppermute | solution.py:13
  20.9 0.1 convert_reduce_fusion.1
  21.1 0.3 fusion.31
  21.4 1.5 all-gather.11.cloned.1.call-done
  22.9 2.1 %copy.40 = bf16[128,8,2,512]{3,1,2,0:T(8,128)(2,1)S(1)} copy(bf16[128,8,2,512]{3,2,1,0:T(2,128)(2,1)} %bitcast.102) | data formatting | bytes 4194304
  25.1 9.6 %all-gather.9.cloned.1.call-done = bf16[1024,512]{1,0:T(8,128)(2,1)} async-done(((bf16[512,512]{1,0:T(8,128)(2,1)}), bf16[1024,512]{1,0:T(8,128)(2,1)}) %all-gather.9.cloned.1.call-update) | async-done | bytes 1048592 | tf_op jit(solution)/shard_map/all_gather | solution.py:31
  34.7 2.4 %fusion.12 = bf16[1,12,24,1536]{3,2,1,0:T(8,128)(2,1)S(1)} fusion(bf16[1024,1024]{1,0:T(8,128)(2,1)S(1)} %bitcast.104, bf16[1024,512]{1,0:T(8,128)(2,1)} %all-gather.9.cloned.1.call-done, bf16[6,24,1024]{2,1,0:T(8,128)(2,1)S(1)} %bitcast.106, bf16[6,24,1024]{2,1,0:T(8,128)(2,1)S(1)} %get-tuple-element.28, f32[12,24]{1,0:T(8,128)S(1)} %add_sqrt_fusion.1, ...), kind=kOutput, calls=%fused_computation.17 | convolution fusion | flops 914178048 | bytes 4622592 | tf_op jit(solution)/shard_map/prcd,de->prce/dot_general | solution.py:48
  37.2 0.2 slice.58
  37.4 1.1 pad_maximum_fusion
  38.5 3.7 %reshape.311 = bf16[1,12,2,12,3,16,32]{6,5,4,3,2,1,0:T(8,128)(2,1)S(1)} reshape(bf16[1,12,24,1536]{3,2,1,0:T(8,128)(2,1)} %pad_maximum_fusion) | data formatting | bytes 1769472 | tf_op jit(solution)/shard_map/reshape | solution.py:53
  42.1 0.6 copy.26
  42.8 0.6 fusion.78
  43.4 1.7 copy.39
  45.1 1.0 copy.38
  46.2 1.0 copy.37
  47.2 4.0 %fusion.81 = (f32[2,16,144]{2,1,0:T(8,128)S(1)}, f32[2,16,144,144]{2,3,1,0:T(8,128)}) fusion(pred[2,144,144]{1,2,0:T(8,128)(4,1)S(1)} %copy-done.8, bf16[1,2,144,1,16,32]{2,5,4,1,3,0:T(8,128)(2,1)S(1)} %copy-done.7, bf16[1,2,144,1,16,32]{2,5,4,1,3,0:T(8,128)(2,1)S(1)} %copy.38), kind=kOutput, calls=%fused_computation.103 | convolution fusion | flops 45121680 | bytes 3303936 | tf_op jit(solution)/shard_map/sub | solution.py:75
  51.2 2.8 %fusion.23 = bf16[1,2,144,16,32]{2,4,3,1,0:T(8,128)(2,1)S(1)} fusion(f32[2,16,144,144]{2,3,1,0:T(8,128)} %get-tuple-element.33, f32[2,16,144]{2,1,0:T(8,128)S(1)} %get-tuple-element.32, bf16[1,2,144,1,16,32]{2,5,4,1,3,0:T(8,128)(2,1)S(1)} %copy.37), kind=kOutput, calls=%fused_computation.37 | convolution fusion | flops 43941888 | bytes 3262464 | tf_op jit(solution)/shard_map/pnhqk,pnkhd->pnqhd/dot_general | solution.py:77
  54.0 1.1 copy.31
  55.1 0.9 reshape.316
  56.0 0.1 copy.32
  56.0 0.1 reshape.317
  56.1 0.1 fusion.70
  56.2 1.8 collective-permute-start.1
  58.0 6.2 %collective-permute-done.1 = bf16[1,6,24,512]{3,2,1,0:T(8,128)(2,1)S(1)} collective-permute-done((bf16[1,6,24,512]{3,2,1,0:T(8,128)(2,1)S(1)}, bf16[1,6,24,512]{3,2,1,0:T(8,128)(2,1)S(1)}, u32[]{:S(2)}, u32[]{:S(2)}) %collective-permute-start.1) | collective-permute-done | bytes 147488 | tf_op jit(solution)/shard_map/ppermute | solution.py:13
  64.1 2.5 %fusion.20 = bf16[1,12,24,1024]{3,2,1,0:T(8,128)(2,1)} fusion(bf16[512,1024]{1,0:T(8,128)(2,1)} %all-gather.13.cloned.1.call-done, bf16[1,12,18,512]{3,2,1,0:T(8,128)(2,1)S(1)} %bitcast.99, bf16[1,12,6,512]{3,2,1,0:T(8,128)(2,1)S(1)} %slice.63, bf16[1,6,24,512]{3,2,1,0:T(8,128)(2,1)S(1)} %collective-permute-done.1), kind=kOutput, calls=%fused_computation.34 | convolution fusion | flops 303169536 | bytes 2080768 | tf_op jit(solution)/shard_map/prce,ed->prcd/dot_general | solution.py:85
  66.7 0.0 all-gather.15.cloned.1.call-start
  66.7 0.5 all-gather.15.cloned.1.call-update
  67.3 0.2 all-gather.21.cloned.1.call-start
  67.5 3.6 %copy.41 = bf16[128,8,2,512]{3,1,2,0:T(8,128)(2,1)} copy(bf16[128,8,2,512]{3,2,1,0:T(2,128)(2,1)} %bitcast.101) | data formatting | bytes 4194304
  71.1 25.1 %all-reduce.2.cloned.1.call-done = bf16[1,12,24,1024]{3,2,1,0:T(8,128)(2,1)} async-done(((bf16[1,12,24,1024]{3,2,1,0:T(8,128)(2,1)}), bf16[1,12,24,1024]{3,2,1,0:T(8,128)(2,1)}) %all-reduce.2.cloned.1.call-update) | async-done | bytes 589840 | tf_op jit(solution)/shard_map/psum | solution.py:88
  96.2 1.5 convert_reduce_fusion
  97.7 0.3 fusion.28
  98.0 0.2 fusion.29
  98.3 1.6 convolution_convert_fusion
  99.9 0.0 all-gather.19.cloned.1.call-start
  99.9 0.7 all-gather.19.cloned.1.call-update
  100.6 0.0 reduce-scatter.2.cloned.1.call-start
  100.7 0.1 convert_reduce_fusion.2
  100.8 0.3 fusion.34
  101.1 5.6 %all-gather.15.cloned.1.call-done = bf16[1024,512]{1,0:T(8,128)(2,1)} async-done(((bf16[512,512]{1,0:T(8,128)(2,1)}), bf16[1024,512]{1,0:T(8,128)(2,1)}) %all-gather.15.cloned.1.call-update) | async-done | bytes 1048592 | tf_op jit(solution)/shard_map/all_gather | solution.py:34
  106.8 1.7 convolution_convert_fusion.3
  108.5 0.8 copy.33
  109.3 50.8 %all-gather.21.cloned.1.call-done = bf16[1152,1024]{1,0:T(8,128)(2,1)} async-done(((bf16[288,1024]{1,0:T(8,128)(2,1)}), bf16[1152,1024]{1,0:T(8,128)(2,1)}) %all-gather.21.cloned.1.call-update) | async-done | bytes 2359312 | tf_op jit(solution)/shard_map/all_gather | solution.py:115
  160.1 1.8 fusion.79
  161.9 0.7 copy.34
  162.6 2.5 %multiply_reduce_fusion = (f32[8,256]{1,0:T(8,128)S(1)}, f32[8,256,1152]{2,1,0:T(8,128)S(1)}) fusion(bf16[256,8,64]{0,2,1:T(8,128)(2,1)} %bitcast.108, bf16[1152,8,64]{0,2,1:T(8,128)(2,1)S(1)} %bitcast.97), kind=kOutput, calls=%fused_computation.2 | convolution fusion | flops 306706432 | bytes 10887168 | tf_op jit(solution)/shard_map/while/body/eval_jaxpr/pqhd,pkhd->phqk/dot_general | solution.py:133
  165.1 1.9 fusion.1
  167.0 1.7 copy-done
  168.7 0.7 copy.35
  169.4 5.5 %fusion.40 = bf16[8,256,64]{1,2,0:T(8,128)(2,1)S(1)} fusion(bf16[1152,8,64]{0,2,1:T(8,128)(2,1)S(1)} %bitcast.105, f32[8,256,1152]{2,1,0:T(8,128)} %copy-done, f32[8,256]{1,0:T(8,128)S(1)} %get-tuple-element.34, f32[8,256]{1,0:T(8,128)S(1)} %get-tuple-element.31, f32[8,256]{1,0:T(8,128)S(1)} %get-tuple-element.30), kind=kOutput, calls=%fused_computation.52 | convolution fusion | flops 309460992 | bytes 10903552 | tf_op jit(solution)/shard_map/while/body/eval_jaxpr/phqk,pkhd->phqd/dot_general | solution.py:140
  175.0 2.5 %fusion.24 = bf16[256,1,1024]{2,0,1:T(8,128)(2,1)} fusion(bf16[256,512]{0,1:T(8,128)(2,1)S(1)} %bitcast.110, bf16[512,1024]{1,0:T(8,128)(2,1)} %all-gather.19.cloned.1.call-done), kind=kOutput, calls=%fused_computation.38 | convolution fusion | flops 268697600 | bytes 1835008 | tf_op jit(solution)/shard_map/pte,ed->tpd/dot_general | solution.py:157
  177.6 13.6 %reduce-scatter.2.cloned.1.call-done = bf16[128,1,1024]{2,0,1:T(8,128)(2,1)} async-done(((bf16[256,1,1024]{2,0,1:T(8,128)(2,1)}), bf16[128,1,1024]{2,0,1:T(8,128)(2,1)}) %reduce-scatter.2.cloned.1.call-update) | async-done | bytes 262160 | tf_op jit(solution)/shard_map/reduce_scatter | solution.py:156
  191.2 1.7 fusion.50
  (40 shorter events, 0.4 us)
Async XLA Ops:
  7.2 2.3 %copy-start.4 = (bf16[1,12,24,1024]{3,2,1,0:T(8,128)(2,1)S(1)}, bf16[1,12,24,1024]{3,2,1,0:T(8,128)(2,1)}, u32[]{:S(2)}) copy-start(bf16[1,12,24,1024]{3,2,1,0:T(8,128)(2,1)} %param.8) | copy-start | bytes 1769476
  7.2 15.8 %all-gather.11.cloned.1.call-start = ((), (), s32[]{:S(2)}) async-start(), calls=%async_computation.2 | async-start | bytes 3145728 | tf_op jit(solution)/shard_map/all_gather | solution.py:32
  7.9 26.8 %all-gather.9.cloned.1.call-start = ((), (), s32[]{:S(2)}) async-start(), calls=%async_computation.1 | async-start | bytes 1572864 | tf_op jit(solution)/shard_map/all_gather | solution.py:31
  8.7 49.3 %all-gather.13.cloned.1.call-start = ((), (), s32[]{:S(2)}) async-start(), calls=%async_computation.3 | async-start | bytes 1572864 | tf_op jit(solution)/shard_map/all_gather | solution.py:33
  9.4 58.1 %all-gather.17.cloned.1.call-start = ((), (), s32[]{:S(2)}) async-start(), calls=%async_computation.6 | async-start | bytes 3145728 | tf_op jit(solution)/shard_map/all_gather | solution.py:35
  9.6 11.4 %collective-permute-start = (bf16[1,6,24,1024]{3,2,1,0:T(8,128)(2,1)S(1)}, bf16[1,6,24,1024]{3,2,1,0:T(8,128)(2,1)S(1)}, u32[]{:S(2)}, u32[]{:S(2)}) collective-permute-start(bf16[1,6,24,1024]{3,2,1,0:T(8,128)(2,1)S(1)} %get-tuple-element.29), channel_id=1, source_target_pairs={{0,12},{4,0},{8,4},{12,8},{1,13},{5,1},{9,5},{13,9},{2,14},{6,2},{... | collective-permute-start | bytes 884744 | tf_op jit(solution)/shard_map/ppermute | solution.py:13
  14.7 81.5 %all-reduce.2.cloned.1.call-start = ((), (), s32[]{:S(2)}) async-start(), calls=%async_computation.4 | async-start | bytes 1179648 | tf_op jit(solution)/shard_map/psum | solution.py:88
  45.1 2.1 %copy-start.7 = (bf16[1,2,144,1,16,32]{2,5,4,1,3,0:T(8,128)(2,1)S(1)}, bf16[1,2,144,1,16,32]{2,5,4,1,3,0:T(8,128)(2,1)}, u32[]{:S(2)}) copy-start(bf16[1,2,144,1,16,32]{2,5,4,1,3,0:T(8,128)(2,1)} %copy.39) | copy-start | bytes 884740
  45.1 2.1 %copy-start.8 = (pred[2,144,144]{1,2,0:T(8,128)(4,1)S(1)}, pred[2,144,144]{1,2,0:T(8,128)(4,1)}, u32[]{:S(2)}) copy-start(pred[2,144,144]{1,2,0:T(8,128)(4,1)} %broadcast_compare_fusion) | copy-start | bytes 124420
  56.2 8.0 %collective-permute-start.1 = (bf16[1,6,24,512]{3,2,1,0:T(8,128)(2,1)S(1)}, bf16[1,6,24,512]{3,2,1,0:T(8,128)(2,1)S(1)}, u32[]{:S(2)}, u32[]{:S(2)}) collective-permute-start(bf16[1,6,24,512]{3,2,1,0:T(8,128)(2,1)S(1)} %fusion.70), channel_id=1, source_target_pairs={{0,4},{4,8},{8,12},{12,0},{1,5},{5,9},{9,13},{13,1},{2,6},{6,10},{... | collective-permute-start | bytes 442376 | tf_op jit(solution)/shard_map/ppermute | solution.py:13
  66.7 40.1 %all-gather.15.cloned.1.call-start = ((), (), s32[]{:S(2)}) async-start(), calls=%async_computation.5 | async-start | bytes 1572864 | tf_op jit(solution)/shard_map/all_gather | solution.py:34
  67.3 92.8 %all-gather.21.cloned.1.call-start = ((), (), s32[]{:S(2)}) async-start(), calls=%async_computation.9 | async-start | bytes 2949120 | tf_op jit(solution)/shard_map/all_gather | solution.py:115
  67.5 28.7 %copy-start.5 = (bf16[1,12,24,1024]{3,2,1,0:T(8,128)(2,1)S(1)}, bf16[1,12,24,1024]{3,2,1,0:T(8,128)(2,1)}, u32[]{:S(2)}) copy-start(bf16[1,12,24,1024]{3,2,1,0:T(8,128)(2,1)} %param.8) | copy-start | bytes 1769476
  96.2 2.0 %copy-start.6 = (bf16[128,8,2,512]{3,1,2,0:T(8,128)(2,1)S(1)}, bf16[128,8,2,512]{3,1,2,0:T(8,128)(2,1)}, u32[]{:S(2)}) copy-start(bf16[128,8,2,512]{3,1,2,0:T(8,128)(2,1)} %copy.41) | copy-start | bytes 6291460
  97.7 2.2 %copy-start.1 = (bf16[1,12,24,1024]{3,2,1,0:T(8,128)(2,1)}, bf16[1,12,24,1024]{3,2,1,0:T(8,128)(2,1)S(1)}, u32[]{:S(2)}) copy-start(bf16[1,12,24,1024]{3,2,1,0:T(8,128)(2,1)S(1)} %get-tuple-element.15) | copy-start | bytes 1769476
  98.2 2.4 %copy-start.2 = (bf16[1,256,1024]{2,1,0:T(8,128)(2,1)S(1)}, bf16[1,256,1024]{2,1,0:T(8,128)(2,1)}, u32[]{:S(2)}) copy-start(bf16[1,256,1024]{2,1,0:T(8,128)(2,1)} %param.9) | copy-start | bytes 1572868
  99.9 75.1 %all-gather.19.cloned.1.call-start = ((), (), s32[]{:S(2)}) async-start(), calls=%async_computation.7 | async-start | bytes 1572864 | tf_op jit(solution)/shard_map/all_gather | solution.py:36
  100.6 90.6 %reduce-scatter.2.cloned.1.call-start = ((), (), s32[]{:S(2)}) async-start(), calls=%async_computation.8 | async-start | bytes 786432 | tf_op jit(solution)/shard_map/reduce_scatter | solution.py:156
  165.1 3.7 %copy-start = (f32[8,256,1152]{2,1,0:T(8,128)}, f32[8,256,1152]{2,1,0:T(8,128)S(1)}, u32[]{:S(2)}) copy-start(f32[8,256,1152]{2,1,0:T(8,128)S(1)} %get-tuple-element.35) | copy-start | bytes 28311556
  175.0 16.3 %copy-start.3 = (bf16[1,256,1024]{2,1,0:T(8,128)(2,1)S(1)}, bf16[1,256,1024]{2,1,0:T(8,128)(2,1)}, u32[]{:S(2)}) copy-start(bf16[1,256,1024]{2,1,0:T(8,128)(2,1)} %param.9) | copy-start | bytes 1572868
Sparse Core Ops, SparseCore 0:
  9.6 13.3 all-gather.10
  24.5 10.1 all-gather.8
  36.3 10.1 all-gather.12
  47.9 11.7 all-gather.16
  66.8 29.3 all-reduce.1
  97.7 9.0 all-gather.14
  108.4 51.6 all-gather.20
  161.7 7.8 all-gather.18
  177.7 13.4 reduce-scatter.1
where the time goes:
time: 200 us; the launch traced here: 199 us
  waiting for transfers between devices  121 us (60%)
  matrix products  25.6 us (13%)
  local copies, waits for them, and re-layouts  22.9 us (11%)
  between operations  14.2 us (7%)
  other arithmetic  8.42 us (4%)
  starting transfers between devices  7.43 us (4%)
    all_gather x1, waiting for transfers between devices, body(): shard_rows = lax.all_gather(page_kv, 'tile', axis=1, tiled=True)  50.8 us
    psum x1, waiting for transfers between devices, body(): lax.psum(partial_proj.astype(jnp.bfloat16), 'mp').astype(jnp.float32)  25.1 us
    reduce_scatter x1, waiting for transfers between devices, body(): lax.psum_scatter(jnp.einsum('pte,ed->tpd', context, wout_dec, preferred_e...  13.6 us
    ppermute x2, waiting for transfers between devices, from_behind(): lax.ppermute(value, axis, [(i, (i + by) % devices) for i in range(devices)])  11.3 us
    unnamed x23, local copies, waits for them, and re-layouts  11.3 us
    all_gather x1, waiting for transfers between devices, body(): lax.all_gather(enc_query, 'batch', axis=0, tiled=True)  9.63 us
    ppermute x2, starting transfers between devices, from_behind(): lax.ppermute(value, axis, [(i, (i + by) % devices) for i in range(devices)])  6.9 us
    all_gather x1, waiting for transfers between devices, body(): lax.all_gather(dec_query, 'batch', axis=0, tiled=True)  5.6 us
  transfers between devices with their start and end apart: 11, of which 8 were waited for; matrix products, arithmetic and copies ran while one was open for 25% of the time, Pallas kernels for 0%

commit v1 on v0

--- a/solution.py
+++ b/solution.py
@@ -112,7 +112,16 @@
         jnp.zeros((pages_here, heads_dec, text_len, HEAD_DEC), jnp.float32),
     )
     carried = start_state
-    shard_rows = lax.all_gather(page_kv, "tile", axis=1, tiled=True)
+    ways = lax.axis_size("tile")
+    up = [(d, (d + 1) % ways) for d in range(ways)]
+    down = [(d, (d - 1) % ways) for d in range(ways)]
+    earlier, later = ([page_kv], [page_kv])
+    for _ in range(ways // 2):
+        earlier.append(lax.ppermute(earlier[-1], "tile", up))
+    for _ in range((ways - 1) // 2):
+        later.append(lax.ppermute(later[-1], "tile", down))
+    line = jnp.concatenate([*earlier[::-1], *later[1:]], axis=1)
+    shard_rows = jnp.roll(line, (lax.axis_index("tile") - ways // 2) * page_kv.shape[1], axis=1)
     count = shard_rows.shape[1] // own_rows
     grouped = max(
         (

time: 200 us -> 184 us (0.920)
  waiting for transfers between devices: 121 us -> 98.1 us
  starting transfers between devices: 7.43 us -> 12.8 us
    all_gather x1 -> x0, waiting for transfers between devices: 50.8 us -> none  [body(): shard_rows = lax.all_gather(page_kv, 'tile', axis=1, tiled=True)]
    ppermute x0 -> x3, waiting for transfers between devices: none -> 35.4 us  [the longest x2 26.4 us: body(): earlier.append(lax.ppermute(earlier[-1], 'tile', up))]
    all_gather x1, waiting for transfers between devices: 5.6 us -> 0.01 us  [body(): lax.all_gather(dec_query, 'batch', axis=0, tiled=True)]
    ppermute x0 -> x3, starting transfers between devices: none -> 5.41 us  [the longest x1 3.87 us: body(): later.append(lax.ppermute(later[-1], 'tile', down))]
    unnamed x23 -> x24, local copies, waits for them, and re-layouts: 11.3 us -> 11.5 us
  transfers between devices with their start and end apart: 11 -> 13, of which waited for: 8 -> 9; matrix products, arithmetic and copies ran while one was open for 25% -> 28% of each run, Pallas kernels for 0% -> 0%
where the time goes in v1:
time: 184 us; the launch traced here: 183 us
  waiting for transfers between devices  98.1 us (53%)
  matrix products  25.8 us (14%)
  local copies, waits for them, and re-layouts  23.3 us (13%)
  between operations  14.6 us (8%)
  starting transfers between devices  12.8 us (7%)
  other arithmetic  8.39 us (5%)
    ppermute x2, waiting for transfers between devices, body(): earlier.append(lax.ppermute(earlier[-1], 'tile', up))  26.4 us
    psum x1, waiting for transfers between devices, body(): lax.psum(partial_proj.astype(jnp.bfloat16), 'mp').astype(jnp.float32)  25.2 us
    reduce_scatter x1, waiting for transfers between devices, body(): lax.psum_scatter(jnp.einsum('pte,ed->tpd', context, wout_dec, preferred_e...  13.4 us
    unnamed x24, local copies, waits for them, and re-layouts  11.5 us
    ppermute x2, waiting for transfers between devices, from_behind(): lax.ppermute(value, axis, [(i, (i + by) % devices) for i in range(devices)])  11.3 us
    all_gather x1, waiting for transfers between devices, body(): lax.all_gather(enc_query, 'batch', axis=0, tiled=True)  9.63 us
    ppermute x1, waiting for transfers between devices, body(): later.append(lax.ppermute(later[-1], 'tile', down))  9 us
    ppermute x2, starting transfers between devices, from_behind(): lax.ppermute(value, axis, [(i, (i + by) % devices) for i in range(devices)])  6.9 us
  transfers between devices with their start and end apart: 13, of which 9 were waited for; matrix products, arithmetic and copies ran while one was open for 28% of the time, Pallas kernels for 0%

profile of v1, /device:TPU:0, one launch (start us, length us, event | category | flops | bytes accessed | tf_op | source)
XLA Modules:
  0.0 183.0 jit_solution(17881215501222349289)
XLA Ops:
  7.2 0.7 all-gather.9.cloned.1.call-update
  7.9 0.7 all-gather.7.cloned.1.call-update
  8.7 0.7 all-gather.11.cloned.1.call-update
  9.4 1.2 fusion.80
  10.6 5.1 %collective-permute-start = (bf16[1,6,24,1024]{3,2,1,0:T(8,128)(2,1)S(1)}, bf16[1,6,24,1024]{3,2,1,0:T(8,128)(2,1)S(1)}, u32[]{:S(2)}, u32[]{:S(2)}) collective-permute-start(bf16[1,6,24,1024]{3,2,1,0:T(8,128)(2,1)S(1)} %get-tuple-element.29), channel_id=1, source_target_pairs={{0,12},{4,0},{8,4},{12,8},{1,13},{5,1},{9,5},{13,9},{2,14},{6,2},{... | collective-permute-start | bytes 884744 | tf_op jit(solution)/shard_map/ppermute | solution.py:13
  15.7 0.0 all-reduce.2.cloned.1.call-start
  15.8 0.1 add.97
  15.9 0.1 add.93
  16.0 0.1 add.94
  16.1 0.7 broadcast_compare_fusion
  16.8 5.1 %collective-permute-done = bf16[1,6,24,1024]{3,2,1,0:T(8,128)(2,1)S(1)} collective-permute-done((bf16[1,6,24,1024]{3,2,1,0:T(8,128)(2,1)S(1)}, bf16[1,6,24,1024]{3,2,1,0:T(8,128)(2,1)S(1)}, u32[]{:S(2)}, u32[]{:S(2)}) %collective-permute-start) | collective-permute-done | bytes 294944 | tf_op jit(solution)/shard_map/ppermute | solution.py:13
  22.0 0.1 convert_reduce_fusion.1
  22.1 0.3 fusion.32
  22.4 0.4 all-gather.9.cloned.1.call-done
  22.9 2.1 %copy.40 = bf16[128,8,2,512]{3,1,2,0:T(8,128)(2,1)S(1)} copy(bf16[128,8,2,512]{3,2,1,0:T(2,128)(2,1)} %bitcast.102) | data formatting | bytes 4194304
  25.0 9.6 %all-gather.7.cloned.1.call-done = bf16[1024,512]{1,0:T(8,128)(2,1)} async-done(((bf16[512,512]{1,0:T(8,128)(2,1)}), bf16[1024,512]{1,0:T(8,128)(2,1)}) %all-gather.7.cloned.1.call-update) | async-done | bytes 1048592 | tf_op jit(solution)/shard_map/all_gather | solution.py:31
  34.6 2.4 %fusion.12 = bf16[1,12,24,1536]{3,2,1,0:T(8,128)(2,1)S(1)} fusion(bf16[1024,1024]{1,0:T(8,128)(2,1)S(1)} %bitcast.104, bf16[1024,512]{1,0:T(8,128)(2,1)} %all-gather.7.cloned.1.call-done, bf16[6,24,1024]{2,1,0:T(8,128)(2,1)S(1)} %bitcast.106, bf16[6,24,1024]{2,1,0:T(8,128)(2,1)S(1)} %get-tuple-element.28, f32[12,24]{1,0:T(8,128)S(1)} %add_sqrt_fusion.1, ...), kind=kOutput, calls=%fused_computation.17 | convolution fusion | flops 914178048 | bytes 4622592 | tf_op jit(solution)/shard_map/prcd,de->prce/dot_general | solution.py:48
  37.1 0.2 slice.58
  37.3 1.1 pad_maximum_fusion
  38.4 3.7 %reshape.311 = bf16[1,12,2,12,3,16,32]{6,5,4,3,2,1,0:T(8,128)(2,1)S(1)} reshape(bf16[1,12,24,1536]{3,2,1,0:T(8,128)(2,1)} %pad_maximum_fusion) | data formatting | bytes 1769472 | tf_op jit(solution)/shard_map/reshape | solution.py:53
  42.0 0.6 copy.26
  42.7 0.6 fusion.79
  43.3 1.7 copy.39
  45.0 1.0 copy.38
  46.1 1.0 copy.37
  47.1 5.0 %fusion.81 = (f32[2,16,144]{2,1,0:T(8,128)S(1)}, f32[2,16,144,144]{2,3,1,0:T(8,128)}) fusion(pred[2,144,144]{1,2,0:T(8,128)(4,1)} %broadcast_compare_fusion, bf16[1,2,144,1,16,32]{2,5,4,1,3,0:T(8,128)(2,1)} %copy.39, bf16[1,2,144,1,16,32]{2,5,4,1,3,0:T(8,128)(2,1)S(1)} %copy.38), kind=kOutput, calls=%fused_computation.113 | convolution fusion | flops 45121680 | bytes 3303936 | tf_op jit(solution)/shard_map/sub | solution.py:75
  52.1 2.8 %fusion.24 = bf16[1,2,144,16,32]{2,4,3,1,0:T(8,128)(2,1)S(1)} fusion(f32[2,16,144,144]{2,3,1,0:T(8,128)} %get-tuple-element.33, f32[2,16,144]{2,1,0:T(8,128)S(1)} %get-tuple-element.32, bf16[1,2,144,1,16,32]{2,5,4,1,3,0:T(8,128)(2,1)S(1)} %copy.37), kind=kOutput, calls=%fused_computation.38 | convolution fusion | flops 43941888 | bytes 3262464 | tf_op jit(solution)/shard_map/pnhqk,pnkhd->pnqhd/dot_general | solution.py:77
  54.9 1.1 copy.31
  56.0 0.9 reshape.316
  56.9 0.1 copy.32
  56.9 0.1 reshape.317
  57.0 0.1 fusion.71
  57.1 1.8 collective-permute-start.1
  58.9 6.2 %collective-permute-done.1 = bf16[1,6,24,512]{3,2,1,0:T(8,128)(2,1)S(1)} collective-permute-done((bf16[1,6,24,512]{3,2,1,0:T(8,128)(2,1)S(1)}, bf16[1,6,24,512]{3,2,1,0:T(8,128)(2,1)S(1)}, u32[]{:S(2)}, u32[]{:S(2)}) %collective-permute-start.1) | collective-permute-done | bytes 147488 | tf_op jit(solution)/shard_map/ppermute | solution.py:13
  65.1 2.5 %fusion.20 = bf16[1,12,24,1024]{3,2,1,0:T(8,128)(2,1)} fusion(bf16[512,1024]{1,0:T(8,128)(2,1)} %all-gather.11.cloned.1.call-done, bf16[1,12,18,512]{3,2,1,0:T(8,128)(2,1)S(1)} %bitcast.100, bf16[1,12,6,512]{3,2,1,0:T(8,128)(2,1)S(1)} %slice.63, bf16[1,6,24,512]{3,2,1,0:T(8,128)(2,1)S(1)} %collective-permute-done.1), kind=kOutput, calls=%fused_computation.34 | convolution fusion | flops 303169536 | bytes 2080768 | tf_op jit(solution)/shard_map/prce,ed->prcd/dot_general | solution.py:85
  67.6 0.0 all-gather.13.cloned.1.call-start
  67.7 0.5 all-gather.13.cloned.1.call-update
  68.2 0.2 all-gather.17.cloned.1.call-start
  68.5 3.5 %copy.41 = bf16[128,8,2,512]{3,1,2,0:T(8,128)(2,1)} copy(bf16[128,8,2,512]{3,2,1,0:T(2,128)(2,1)} %bitcast.101) | data formatting | bytes 4194304
  72.0 25.2 %all-reduce.2.cloned.1.call-done = bf16[1,12,24,1024]{3,2,1,0:T(8,128)(2,1)} async-done(((bf16[1,12,24,1024]{3,2,1,0:T(8,128)(2,1)}), bf16[1,12,24,1024]{3,2,1,0:T(8,128)(2,1)}) %all-reduce.2.cloned.1.call-update) | async-done | bytes 589840 | tf_op jit(solution)/shard_map/psum | solution.py:88
  97.1 1.5 convert_reduce_fusion
  98.6 0.3 fusion.29
  98.9 0.2 fusion.30
  99.2 0.8 fusion.21
  100.0 1.5 collective-permute-start.2
  101.5 0.0 reduce-scatter.2.cloned.1.call-start
  101.6 0.1 convert_reduce_fusion.2
  101.8 15.1 %collective-permute-done.2 = bf16[1,288,1024]{2,1,0:T(8,128)(2,1)S(1)} collective-permute-done((bf16[1,288,1024]{2,1,0:T(8,128)(2,1)S(1)}, bf16[1,288,1024]{2,1,0:T(8,128)(2,1)S(1)}, u32[]{:S(2)}, u32[]{:S(2)}) %collective-permute-start.2) | collective-permute-done | bytes 589856 | tf_op jit(solution)/shard_map/ppermute | solution.py:120
  116.9 0.3 fusion.35
  117.2 3.9 %collective-permute-start.4 = (bf16[1,288,1024]{2,1,0:T(8,128)(2,1)S(1)}, bf16[1,288,1024]{2,1,0:T(8,128)(2,1)S(1)}, u32[]{:S(2)}, u32[]{:S(2)}) collective-permute-start(bf16[1,288,1024]{2,1,0:T(8,128)(2,1)S(1)} %fusion.21), channel_id=1, source_target_pairs={{0,12},{4,0},{8,4},{12,8},{1,13},{5,1},{9,5},{13,9},{2,14},{6,2},{... | collective-permute-start | bytes 1769480 | tf_op jit(solution)/shard_map/ppermute | solution.py:122
  121.1 1.7 convolution_convert_fusion.3
  122.8 0.8 copy.33
  123.6 11.3 %collective-permute-done.3 = bf16[1,288,1024]{2,1,0:T(8,128)(2,1)S(1)} collective-permute-done((bf16[1,288,1024]{2,1,0:T(8,128)(2,1)S(1)}, bf16[1,288,1024]{2,1,0:T(8,128)(2,1)S(1)}, u32[]{:S(2)}, u32[]{:S(2)}) %collective-permute-start.3) | collective-permute-done | bytes 589856 | tf_op jit(solution)/shard_map/ppermute | solution.py:120
  135.1 9.0 %collective-permute-done.4 = bf16[1,288,1024]{2,1,0:T(8,128)(2,1)S(1)} collective-permute-done((bf16[1,288,1024]{2,1,0:T(8,128)(2,1)S(1)}, bf16[1,288,1024]{2,1,0:T(8,128)(2,1)S(1)}, u32[]{:S(2)}, u32[]{:S(2)}) %collective-permute-start.4) | collective-permute-done | bytes 589856 | tf_op jit(solution)/shard_map/ppermute | solution.py:122
  144.3 1.0 constant_dynamic-slice_fusion
  145.3 0.7 copy.34
  146.0 2.5 %multiply_reduce_fusion = (f32[8,256]{1,0:T(8,128)S(1)}, f32[8,256,1152]{2,1,0:T(8,128)S(1)}) fusion(bf16[256,8,64]{0,2,1:T(8,128)(2,1)} %bitcast.108, bf16[1152,8,64]{0,2,1:T(8,128)(2,1)S(1)} %bitcast.98), kind=kOutput, calls=%fused_computation.2 | convolution fusion | flops 306706432 | bytes 10887168 | tf_op jit(solution)/shard_map/while/body/eval_jaxpr/pqhd,pkhd->phqk/dot_general | solution.py:142
  148.5 1.9 %fusion.1 = f32[8,256]{1,0:T(8,128)S(1)} fusion(f32[8,256,1152]{2,1,0:T(8,128)S(1)} %get-tuple-element.35, f32[8,256]{1,0:T(8,128)S(1)} %get-tuple-element.34), kind=kLoop, calls=%fused_computation.3 | loop fusion | flops 7075840 | bytes 9453568 | tf_op jit(solution)/shard_map/while/body/eval_jaxpr/reduce_sum | solution.py:148
  150.4 1.7 copy-done
  152.1 0.7 copy.35
  152.9 5.6 %fusion.41 = bf16[8,256,64]{1,2,0:T(8,128)(2,1)S(1)} fusion(bf16[1152,8,64]{0,2,1:T(8,128)(2,1)S(1)} %bitcast.105, f32[8,256,1152]{2,1,0:T(8,128)} %copy-done, f32[8,256]{1,0:T(8,128)S(1)} %get-tuple-element.34, f32[8,256]{1,0:T(8,128)S(1)} %get-tuple-element.31, f32[8,256]{1,0:T(8,128)S(1)} %get-tuple-element.30), kind=kOutput, calls=%fused_computation.53 | convolution fusion | flops 309460992 | bytes 10903552 | tf_op jit(solution)/shard_map/while/body/eval_jaxpr/phqk,pkhd->phqd/dot_general | solution.py:149
  158.5 2.5 %fusion.25 = bf16[256,1,1024]{2,0,1:T(8,128)(2,1)} fusion(bf16[256,512]{0,1:T(8,128)(2,1)S(1)} %bitcast.110, bf16[512,1024]{1,0:T(8,128)(2,1)} %all-gather.17.cloned.1.call-done), kind=kOutput, calls=%fused_computation.39 | convolution fusion | flops 268697600 | bytes 1835008 | tf_op jit(solution)/shard_map/pte,ed->tpd/dot_general | solution.py:166
  161.0 13.4 %reduce-scatter.2.cloned.1.call-done = bf16[128,1,1024]{2,0,1:T(8,128)(2,1)} async-done(((bf16[256,1,1024]{2,0,1:T(8,128)(2,1)}), bf16[128,1,1024]{2,0,1:T(8,128)(2,1)}) %reduce-scatter.2.cloned.1.call-update) | async-done | bytes 262160 | tf_op jit(solution)/shard_map/reduce_scatter | solution.py:165
  174.4 1.7 fusion.51
  (45 shorter events, 0.7 us)
Async XLA Ops:
  7.2 15.7 %all-gather.9.cloned.1.call-start = ((), (), s32[]{:S(2)}) async-start(), calls=%async_computation.2 | async-start | bytes 3145728 | tf_op jit(solution)/shard_map/all_gather | solution.py:32
  7.9 26.7 %all-gather.7.cloned.1.call-start = ((), (), s32[]{:S(2)}) async-start(), calls=%async_computation.1 | async-start | bytes 1572864 | tf_op jit(solution)/shard_map/all_gather | solution.py:31
  8.6 50.3 %all-gather.11.cloned.1.call-start = ((), (), s32[]{:S(2)}) async-start(), calls=%async_computation.3 | async-start | bytes 1572864 | tf_op jit(solution)/shard_map/all_gather | solution.py:33
  9.4 59.1 %all-gather.15.cloned.1.call-start = ((), (), s32[]{:S(2)}) async-start(), calls=%async_computation.6 | async-start | bytes 3145728 | tf_op jit(solution)/shard_map/all_gather | solution.py:35
  10.6 11.4 %collective-permute-start = (bf16[1,6,24,1024]{3,2,1,0:T(8,128)(2,1)S(1)}, bf16[1,6,24,1024]{3,2,1,0:T(8,128)(2,1)S(1)}, u32[]{:S(2)}, u32[]{:S(2)}) collective-permute-start(bf16[1,6,24,1024]{3,2,1,0:T(8,128)(2,1)S(1)} %get-tuple-element.29), channel_id=1, source_target_pairs={{0,12},{4,0},{8,4},{12,8},{1,13},{5,1},{9,5},{13,9},{2,14},{6,2},{... | collective-permute-start | bytes 884744 | tf_op jit(solution)/shard_map/ppermute | solution.py:13
  15.7 81.4 %all-reduce.2.cloned.1.call-start = ((), (), s32[]{:S(2)}) async-start(), calls=%async_computation.4 | async-start | bytes 1179648 | tf_op jit(solution)/shard_map/psum | solution.py:88
  57.1 40.0 %copy-start.4 = (bf16[1,12,24,1024]{3,2,1,0:T(8,128)(2,1)S(1)}, bf16[1,12,24,1024]{3,2,1,0:T(8,128)(2,1)}, u32[]{:S(2)}) copy-start(bf16[1,12,24,1024]{3,2,1,0:T(8,128)(2,1)} %param.8) | copy-start | bytes 1769476
  57.1 8.0 %collective-permute-start.1 = (bf16[1,6,24,512]{3,2,1,0:T(8,128)(2,1)S(1)}, bf16[1,6,24,512]{3,2,1,0:T(8,128)(2,1)S(1)}, u32[]{:S(2)}, u32[]{:S(2)}) collective-permute-start(bf16[1,6,24,512]{3,2,1,0:T(8,128)(2,1)S(1)} %fusion.71), channel_id=1, source_target_pairs={{0,4},{4,8},{8,12},{12,0},{1,5},{5,9},{9,13},{13,1},{2,6},{6,10},{... | collective-permute-start | bytes 442376 | tf_op jit(solution)/shard_map/ppermute | solution.py:13
  67.6 53.5 %all-gather.13.cloned.1.call-start = ((), (), s32[]{:S(2)}) async-start(), calls=%async_computation.5 | async-start | bytes 1572864 | tf_op jit(solution)/shard_map/all_gather | solution.py:34
  68.2 90.3 %all-gather.17.cloned.1.call-start = ((), (), s32[]{:S(2)}) async-start(), calls=%async_computation.7 | async-start | bytes 1572864 | tf_op jit(solution)/shard_map/all_gather | solution.py:36
  97.1 2.0 %copy-start.5 = (bf16[128,8,2,512]{3,1,2,0:T(8,128)(2,1)S(1)}, bf16[128,8,2,512]{3,1,2,0:T(8,128)(2,1)}, u32[]{:S(2)}) copy-start(bf16[128,8,2,512]{3,1,2,0:T(8,128)(2,1)} %copy.41) | copy-start | bytes 6291460
  98.6 2.9 %copy-start.1 = (bf16[1,12,24,1024]{3,2,1,0:T(8,128)(2,1)}, bf16[1,12,24,1024]{3,2,1,0:T(8,128)(2,1)S(1)}, u32[]{:S(2)}) copy-start(bf16[1,12,24,1024]{3,2,1,0:T(8,128)(2,1)S(1)} %get-tuple-element.15) | copy-start | bytes 1769476
  98.9 2.7 %copy-start.2 = (bf16[1,256,1024]{2,1,0:T(8,128)(2,1)S(1)}, bf16[1,256,1024]{2,1,0:T(8,128)(2,1)}, u32[]{:S(2)}) copy-start(bf16[1,256,1024]{2,1,0:T(8,128)(2,1)} %param.9) | copy-start | bytes 1572868
  100.0 16.9 %collective-permute-start.2 = (bf16[1,288,1024]{2,1,0:T(8,128)(2,1)S(1)}, bf16[1,288,1024]{2,1,0:T(8,128)(2,1)S(1)}, u32[]{:S(2)}, u32[]{:S(2)}) collective-permute-start(bf16[1,288,1024]{2,1,0:T(8,128)(2,1)S(1)} %fusion.21), channel_id=1, source_target_pairs={{0,4},{4,8},{8,12},{12,0},{1,5},{5,9},{9,13},{13,1},{2,6},{6,10},{... | collective-permute-start | bytes 1769480 | tf_op jit(solution)/shard_map/ppermute | solution.py:120
  101.5 72.9 %reduce-scatter.2.cloned.1.call-start = ((), (), s32[]{:S(2)}) async-start(), calls=%async_computation.8 | async-start | bytes 786432 | tf_op jit(solution)/shard_map/reduce_scatter | solution.py:165
  116.9 18.1 %collective-permute-start.3 = (bf16[1,288,1024]{2,1,0:T(8,128)(2,1)S(1)}, bf16[1,288,1024]{2,1,0:T(8,128)(2,1)S(1)}, u32[]{:S(2)}, u32[]{:S(2)}) collective-permute-start(bf16[1,288,1024]{2,1,0:T(8,128)(2,1)S(1)} %collective-permute-done.2), channel_id=1, source_target_pairs={{0,4},{4,8},{8,12},{12,0},{1,5},{5,9},{9,13},{13,1},{2,6},{6,10},{... | collective-permute-start | bytes 1769480 | tf_op jit(solution)/shard_map/ppermute | solution.py:120
  117.2 26.9 %collective-permute-start.4 = (bf16[1,288,1024]{2,1,0:T(8,128)(2,1)S(1)}, bf16[1,288,1024]{2,1,0:T(8,128)(2,1)S(1)}, u32[]{:S(2)}, u32[]{:S(2)}) collective-permute-start(bf16[1,288,1024]{2,1,0:T(8,128)(2,1)S(1)} %fusion.21), channel_id=1, source_target_pairs={{0,12},{4,0},{8,4},{12,8},{1,13},{5,1},{9,5},{13,9},{2,14},{6,2},{... | collective-permute-start | bytes 1769480 | tf_op jit(solution)/shard_map/ppermute | solution.py:122
  148.5 3.6 %copy-start = (f32[8,256,1152]{2,1,0:T(8,128)}, f32[8,256,1152]{2,1,0:T(8,128)S(1)}, u32[]{:S(2)}) copy-start(f32[8,256,1152]{2,1,0:T(8,128)S(1)} %get-tuple-element.35) | copy-start | bytes 28311556
  152.9 21.6 %copy-start.3 = (bf16[1,256,1024]{2,1,0:T(8,128)(2,1)S(1)}, bf16[1,256,1024]{2,1,0:T(8,128)(2,1)}, u32[]{:S(2)}) copy-start(bf16[1,256,1024]{2,1,0:T(8,128)(2,1)} %param.9) | copy-start | bytes 1572868
Sparse Core Ops, SparseCore 0:
  9.5 13.2 all-gather.8
  24.4 10.1 all-gather.6
  36.2 10.1 all-gather.10
  47.8 11.7 all-gather.14
  67.7 29.3 all-reduce.1
  98.6 9.0 all-gather.12
  109.3 10.1 all-gather.16
  161.1 13.2 reduce-scatter.1
